TPU v7x, 32 devices: a whole 2x2x4 slice. The times are simulated.
32 devices in a mesh: row: 8 (over z, x), col: 4 (over y, core).
Axes of the slice: x: 2, y: 2, z: 4, core: 2. Of those that a mesh axis runs over, the one named last changes fastest.
Arguments:
- mel: float32 [128, 18432], P('col', 'row'), may hold values from -6 to 6
- pair_val: int32 [128], replicated, may hold values from 0 to 31
- pair_cond: int32 [128], replicated, may hold values from 0 to 31
- val_energy: float32 [32], replicated, may hold values from -8 to -1
- cond_energy: float32 [32], replicated, may hold values from 1 to 8
- freqs: float32 [2], replicated, may hold values from 0.5 to 6
Outputs:
- chi: float32 [2, 18432, 18432], P(None, 'row', 'col')
All inputs are finite; a program needn't handle non-finite values.
Results may differ from a plain program's by a relative error of at most 0.000098.
Values sent between devices are 32-bit elements; how exact they have to be, the bound alone decides.
A program may use at most 128 MiB of HBM per device.

v0:
```python
import math
import jax
import jax.numpy as jnp
from jax import lax
from jax.sharding import PartitionSpec as P

PAIRS = 128


def body(mel, pair_val, pair_cond, val_energy, cond_energy, freqs):
    rows_all = lax.all_gather(mel, "col", axis=0, tiled=True)
    own_block = lax.all_gather(mel, "row", axis=1, tiled=True)
    col_block = lax.all_to_all(own_block, "col", split_axis=1, concat_axis=0, tiled=True)
    cond_onehot = (
        pair_cond[:, None] == jnp.arange(cond_energy.shape[0], dtype=jnp.int32)[None, :]
    ).astype(jnp.float32)
    val_onehot = (
        pair_val[:, None] == jnp.arange(val_energy.shape[0], dtype=jnp.int32)[None, :]
    ).astype(jnp.float32)
    gap = jnp.sum(cond_onehot * cond_energy[None, :], axis=1) - jnp.sum(
        val_onehot * val_energy[None, :], axis=1
    )
    scale = 1.0 / math.sqrt(PAIRS)
    weights = (
        -4.0
        * gap[None, :]
        / (gap[None, :] * gap[None, :] + freqs[:, None] * freqs[:, None])
        * scale
    )
    scaled = weights[:, :, None] * rows_all[None, :, :]
    return lax.dot_general(
        scaled,
        col_block,
        (((1,), (0,)), ((), ())),
        precision=lax.Precision.HIGHEST,
        preferred_element_type=jnp.float32,
    )


def solution(mesh):
    return jax.shard_map(
        body,
        mesh=mesh,
        in_specs=(P("col", "row"), P(), P(), P(), P(), P()),
        out_specs=P(None, "row", "col"),
        check_vma=False,
    )
```

profile of v0, /device:TPU:0, one launch (start us, length us, event | category | flops | bytes accessed | tf_op | source)
XLA Modules:
  0.0 184.6 jit_solution(5742177264491357623)
XLA Ops:
  6.5 0.0 all-gather.5.cloned.1.call-start
  6.5 0.7 all-gather.5.cloned.1.call-update
  7.3 0.0 all-gather.3.cloned.1.call-start
  7.3 0.7 all-gather.3.cloned.1.call-update
  8.0 56.1 %all-gather.5.cloned.1.call-done = f32[32,18432]{1,0:T(8,128)} async-done(((f32[32,2304]{1,0:T(8,128)}), f32[32,18432]{1,0:T(8,128)}) %all-gather.5.cloned.1.call-update) | async-done | bytes 2359312 | tf_op jit(solution)/shard_map/all_gather | solution.py:12
  64.1 3.2 %copy.13 = f32[4,4,8,4608]{3,2,0,1:T(8,128)} copy(f32[4,4,8,4608]{3,2,1,0:T(8,128)} %bitcast.13) | data formatting | bytes 4718592 | tf_op jit(solution)/shard_map/all_to_all | solution.py:13
  67.3 0.0 copy-start.4
  67.3 0.0 copy-start
  67.3 0.0 copy-start.1
  67.3 0.0 copy-start.2
  67.3 0.0 copy-start.3
  67.4 3.8 %all-to-all-start = ((f32[32,4,4608]{2,0,1:T(8,128)}), f32[32,4,4608]{2,0,1:T(8,128)S(1)}, u32[]{:S(2)}, u32[]{:S(2)}) async-start(f32[32,4,4608]{2,0,1:T(8,128)} %bitcast.12), calls=%async_computation | async-start | bytes 4718592 | tf_op jit(solution)/shard_map/all_to_all | solution.py:13
  71.2 0.0 copy-done.4
  71.2 0.0 copy-done
  71.2 0.0 copy-done.1
  71.2 0.0 copy-done.2
  71.2 0.0 copy-done.3
  71.2 0.1 select_reduce_fusion
  71.3 0.1 divide_multiply_fusion
  71.4 16.4 %all-gather.3.cloned.1.call-done = f32[128,2304]{1,0:T(8,128)} async-done(((f32[32,2304]{1,0:T(8,128)}), f32[128,2304]{1,0:T(8,128)}) %all-gather.3.cloned.1.call-update) | async-done | bytes 1179664 | tf_op jit(solution)/shard_map/all_gather | solution.py:11
  87.8 1.6 copy.9
  89.4 16.0 %all-to-all-done = f32[32,4,4608]{2,0,1:T(8,128)S(1)} async-done(((f32[32,4,4608]{2,0,1:T(8,128)}), f32[32,4,4608]{2,0,1:T(8,128)S(1)}, u32[]{:S(2)}, u32[]{:S(2)}) %all-to-all-start) | async-done | bytes 2359328 | tf_op jit(solution)/shard_map/all_to_all | solution.py:13
  105.4 72.3 %fusion = f32[2,2304,4608]{2,1,0:T(8,128)} fusion(f32[128,4608,1]{1,0,2:T(8,128)S(1)} %bitcast.11, f32[128,2304]{0,1:T(8,128)S(1)} %copy.9, f32[2,128]{1,0:T(2,128)S(1)} %divide_multiply_fusion), kind=kOutput, calls=%fused_computation.1 | convolution fusion | flops 32615497728 | bytes 88474624 | tf_op jit(solution)/shard_map/dot_general | solution.py:31
  (2 shorter events, 0.0 us)
Async XLA Ops:
  6.5 57.6 %all-gather.5.cloned.1.call-start = ((), (), s32[]{:S(2)}) async-start(), calls=%async_computation.2 | async-start | bytes 2654208 | tf_op jit(solution)/shard_map/all_gather | solution.py:12
  7.3 80.5 %all-gather.3.cloned.1.call-start = ((), (), s32[]{:S(2)}) async-start(), calls=%async_computation.1 | async-start | bytes 1474560 | tf_op jit(solution)/shard_map/all_gather | solution.py:11
  67.3 3.8 %copy-start.4 = (f32[2]{0:T(128)S(1)}, f32[2]{0:T(128)}, u32[]{:S(2)}) copy-start(f32[2]{0:T(128)} %param.11) | copy-start | bytes 28
  67.3 3.8 %copy-start = (f32[32]{0:T(128)S(1)}, f32[32]{0:T(128)}, u32[]{:S(2)}) copy-start(f32[32]{0:T(128)} %param.9) | copy-start | bytes 388
  67.3 3.9 %copy-start.1 = (s32[128]{0:T(128)S(1)}, s32[128]{0:T(128)}, u32[]{:S(2)}) copy-start(s32[128]{0:T(128)} %param.7) | copy-start | bytes 1540
  67.3 3.9 %copy-start.2 = (f32[32]{0:T(128)S(1)}, f32[32]{0:T(128)}, u32[]{:S(2)}) copy-start(f32[32]{0:T(128)} %param.10) | copy-start | bytes 388
  67.3 3.9 %copy-start.3 = (s32[128]{0:T(128)S(1)}, s32[128]{0:T(128)}, u32[]{:S(2)}) copy-start(s32[128]{0:T(128)} %param.8) | copy-start | bytes 1540
  67.4 38.1 %all-to-all-start = ((f32[32,4,4608]{2,0,1:T(8,128)}), f32[32,4,4608]{2,0,1:T(8,128)S(1)}, u32[]{:S(2)}, u32[]{:S(2)}) async-start(f32[32,4,4608]{2,0,1:T(8,128)} %bitcast.12), calls=%async_computation | async-start | bytes 4718592 | tf_op jit(solution)/shard_map/all_to_all | solution.py:13
Sparse Core Ops, SparseCore 0:
  9.5 54.5 all-gather.4
  65.7 22.0 all-gather.2
where the time goes:
time: 185 us
  waiting for transfers between devices  89.9 us (49%)
  matrix products  72.3 us (39%)
  between operations  13.5 us (7%)
  local copies, waits for them, and re-layouts  4.89 us (3%)
  starting transfers between devices  3.84 us (2%)
    dot_general x1, matrix products, body(): lax.dot_general(scaled, col_block, (((1,), (0,)), ((), ())), precision=la...  72.3 us
    all_gather x1, waiting for transfers between devices, body(): own_block = lax.all_gather(mel, 'row', axis=1, tiled=True)  56.1 us
    all_gather x1, waiting for transfers between devices, body(): rows_all = lax.all_gather(mel, 'col', axis=0, tiled=True)  16.4 us
    all_to_all x1, waiting for transfers between devices, body(): lax.all_to_all(own_block, 'col', split_axis=1, concat_axis=0, tiled=True)  16 us
    all_to_all x1, starting transfers between devices, body(): lax.all_to_all(own_block, 'col', split_axis=1, concat_axis=0, tiled=True)  3.8 us
  transfers between devices with their start and end apart: 3, of which 3 were waited for; matrix products, arithmetic and copies ran while one was open for 3% of the time, Pallas kernels for 0%

commit v1 on v0

--- a/solution.py
+++ b/solution.py
@@ -8,7 +8,16 @@
 
 
 def body(mel, pair_val, pair_cond, val_energy, cond_energy, freqs):
-    rows_all = lax.all_gather(mel, "col", axis=0, tiled=True)
+    num_devices = jax.lax.axis_size("col")
+    then = sorted(((pp, (pp + 1) % num_devices) for pp in range(num_devices)))
+    carry_out = mel
+    pages = [carry_out]
+    for p in tuple(range(1, num_devices)):
+        carry_out = jax.lax.ppermute(carry_out, "col", then)
+        pages.insert(0, carry_out)
+    heard = jnp.concatenate(pages, 0)
+    carry = jax.lax.axis_index("col") + 1
+    rows_all = jnp.roll(heard, carry * mel.shape[0], 0)
     own_block = lax.all_gather(mel, "row", axis=1, tiled=True)
     col_block = lax.all_to_all(own_block, "col", split_axis=1, concat_axis=0, tiled=True)
     cond_onehot = (

time: 185 us -> 179 us (0.968)
  waiting for transfers between devices: 89.9 us -> 73.9 us
  local copies, waits for them, and re-layouts: 4.89 us -> 13.1 us
    all_gather x1, waiting for transfers between devices: 56.1 us -> 35.2 us  [body(): own_block = lax.all_gather(mel, 'row', axis=1, tiled=True)]
    ppermute x0 -> x3, waiting for transfers between devices: none -> 17.2 us  [body(): carry_out = jax.lax.ppermute(carry_out, 'col', then)]
    all_gather x1 -> x0, waiting for transfers between devices: 16.4 us -> none  [body(): rows_all = lax.all_gather(mel, 'col', axis=0, tiled=True)]
    unnamed x10 -> x9, local copies, waits for them, and re-layouts: 0.02 us -> 5.15 us
    all_to_all x1, waiting for transfers between devices: 16 us -> 20.8 us  [body(): lax.all_to_all(own_block, 'col', split_axis=1, concat_axis=0, tiled=True)]
    dynamic_slice x0 -> x2, local copies, waits for them, and re-layouts: none -> 3.98 us  [body(): rows_all = jnp.roll(heard, carry * mel.shape[0], 0)]
  transfers between devices with their start and end apart: 3 -> 5, of which waited for: 3 -> 5; matrix products, arithmetic and copies ran while one was open for 3% -> 6% of each run, Pallas kernels for 0% -> 0%
where the time goes in v1:
time: 179 us
  waiting for transfers between devices  73.9 us (41%)
  matrix products  72.3 us (40%)
  between operations  13.4 us (7%)
  local copies, waits for them, and re-layouts  13.1 us (7%)
  starting transfers between devices  4.35 us (2%)
    dot_general x1, matrix products, body(): lax.dot_general(scaled, col_block, (((1,), (0,)), ((), ())), precision=la...  72.3 us
    all_gather x1, waiting for transfers between devices, body(): own_block = lax.all_gather(mel, 'row', axis=1, tiled=True)  35.2 us
    all_to_all x1, waiting for transfers between devices, body(): lax.all_to_all(own_block, 'col', split_axis=1, concat_axis=0, tiled=True)  20.8 us
    ppermute x3, waiting for transfers between devices, body(): carry_out = jax.lax.ppermute(carry_out, 'col', then)  17.2 us
    unnamed x9, local copies, waits for them, and re-layouts  5.15 us
    dynamic_slice x2, local copies, waits for them, and re-layouts, body(): rows_all = jnp.roll(heard, carry * mel.shape[0], 0)  3.98 us
    all_to_all x1, starting transfers between devices, body(): lax.all_to_all(own_block, 'col', split_axis=1, concat_axis=0, tiled=True)  3.76 us
  transfers between devices with their start and end apart: 5, of which 5 were waited for; matrix products, arithmetic and copies ran while one was open for 6% of the time, Pallas kernels for 0%

profile of v1, /device:TPU:0, one launch (start us, length us, event | category | flops | bytes accessed | tf_op | source)
XLA Modules:
  0.0 178.7 jit_solution(10945525864663286185)
XLA Ops:
  6.5 0.0 all-gather.2.cloned.1.call-start
  6.5 0.7 all-gather.2.cloned.1.call-update
  7.3 0.5 collective-permute-start
  7.8 6.6 %collective-permute-done = f32[32,2304]{1,0:T(8,128)S(1)} collective-permute-done((f32[32,2304]{1,0:T(8,128)}, f32[32,2304]{1,0:T(8,128)S(1)}, u32[]{:S(2)}, u32[]{:S(2)}) %collective-permute-start) | collective-permute-done | bytes 294944 | tf_op jit(solution)/shard_map/ppermute | solution.py:16
  14.4 0.0 collective-permute-start.1
  14.4 0.8 select_reduce_fusion
  15.2 5.3 %collective-permute-done.1 = f32[32,2304]{1,0:T(8,128)S(1)} collective-permute-done((f32[32,2304]{1,0:T(8,128)S(1)}, f32[32,2304]{1,0:T(8,128)S(1)}, u32[]{:S(2)}, u32[]{:S(2)}) %collective-permute-start.1) | collective-permute-done | bytes 294944 | tf_op jit(solution)/shard_map/ppermute | solution.py:16
  20.5 0.0 collective-permute-start.2
  20.5 0.7 mul.72
  21.3 0.1 divide_multiply_fusion
  21.3 5.3 %collective-permute-done.2 = f32[32,2304]{1,0:T(8,128)S(1)} collective-permute-done((f32[32,2304]{1,0:T(8,128)S(1)}, f32[32,2304]{1,0:T(8,128)S(1)}, u32[]{:S(2)}, u32[]{:S(2)}) %collective-permute-start.2) | collective-permute-done | bytes 294944 | tf_op jit(solution)/shard_map/ppermute | solution.py:16
  26.7 0.7 constant_dynamic-update-slice_fusion.7
  27.4 0.7 constant_dynamic-update-slice_fusion.6
  28.1 0.7 constant_dynamic-update-slice_fusion.5
  28.9 35.2 %all-gather.2.cloned.1.call-done = f32[32,18432]{1,0:T(8,128)} async-done(((f32[32,2304]{1,0:T(8,128)}), f32[32,18432]{1,0:T(8,128)}) %all-gather.2.cloned.1.call-update) | async-done | bytes 2359312 | tf_op jit(solution)/shard_map/all_gather | solution.py:21
  64.1 3.2 %copy.13 = f32[4,4,8,4608]{3,2,0,1:T(8,128)} copy(f32[4,4,8,4608]{3,2,1,0:T(8,128)} %bitcast.13) | data formatting | bytes 4718592 | tf_op jit(solution)/shard_map/all_to_all | solution.py:22
  67.3 0.0 copy-start
  67.3 3.8 %all-to-all-start = ((f32[32,4,4608]{2,0,1:T(8,128)}), f32[32,4,4608]{2,0,1:T(8,128)S(1)}, u32[]{:S(2)}, u32[]{:S(2)}) async-start(f32[32,4,4608]{2,0,1:T(8,128)} %bitcast.12), calls=%async_computation | async-start | bytes 4718592 | tf_op jit(solution)/shard_map/all_to_all | solution.py:22
  71.1 0.0 copy-done
  71.1 0.7 constant_dynamic-update-slice_fusion.4
  71.9 0.7 constant_dynamic-update-slice_fusion.3
  72.6 0.7 constant_dynamic-update-slice_fusion.2
  73.3 0.7 constant_dynamic-update-slice_fusion.1
  74.0 0.8 constant_dynamic-update-slice_fusion
  74.8 2.4 %constant_dynamic-slice_fusion = f32[128,2304]{1,0:T(8,128)} fusion(f32[256,2304]{1,0:T(8,128)} %constant_dynamic-update-slice_fusion, s32[]{:T(128)S(6)} %select_n.14), kind=kLoop, calls=%fused_computation.18 | loop fusion | bytes 2359300 | tf_op jit(solution)/shard_map/jit(_roll_dynamic)/dynamic_slice | solution.py:20
  77.1 1.6 copy.9
  78.8 20.8 %all-to-all-done = f32[32,4,4608]{2,0,1:T(8,128)S(1)} async-done(((f32[32,4,4608]{2,0,1:T(8,128)}), f32[32,4,4608]{2,0,1:T(8,128)S(1)}, u32[]{:S(2)}, u32[]{:S(2)}) %all-to-all-start) | async-done | bytes 2359328 | tf_op jit(solution)/shard_map/all_to_all | solution.py:22
  99.6 72.3 %fusion = f32[2,2304,4608]{2,1,0:T(8,128)} fusion(f32[128,4608,1]{1,0,2:T(8,128)S(1)} %bitcast.11, f32[128,2304]{0,1:T(8,128)S(1)} %copy.9, f32[2,128]{1,0:T(2,128)S(1)} %divide_multiply_fusion), kind=kOutput, calls=%fused_computation.1 | convolution fusion | flops 32615497728 | bytes 88474624 | tf_op jit(solution)/shard_map/dot_general | solution.py:40
  (1 shorter events, 0.0 us)
Async XLA Ops:
  6.5 57.6 %all-gather.2.cloned.1.call-start = ((), (), s32[]{:S(2)}) async-start(), calls=%async_computation.1 | async-start | bytes 2654208 | tf_op jit(solution)/shard_map/all_gather | solution.py:21
  7.3 7.1 %collective-permute-start = (f32[32,2304]{1,0:T(8,128)}, f32[32,2304]{1,0:T(8,128)S(1)}, u32[]{:S(2)}, u32[]{:S(2)}) collective-permute-start(f32[32,2304]{1,0:T(8,128)} %param.6), channel_id=1, source_target_pairs={{0,1},{1,2},{2,3},{3,0},{4,5},{5,6},{6,7},{7,4},{8,9},{9,10},{10,1... | collective-permute-start | bytes 884744 | tf_op jit(solution)/shard_map/ppermute | solution.py:16
  14.4 6.1 %collective-permute-start.1 = (f32[32,2304]{1,0:T(8,128)S(1)}, f32[32,2304]{1,0:T(8,128)S(1)}, u32[]{:S(2)}, u32[]{:S(2)}) collective-permute-start(f32[32,2304]{1,0:T(8,128)S(1)} %collective-permute-done), channel_id=1, source_target_pairs={{0,1},{1,2},{2,3},{3,0},{4,5},{5,6},{6,7},{7,4},{8,9},{9,10},{10,1... | collective-permute-start | bytes 884744 | tf_op jit(solution)/shard_map/ppermute | solution.py:16
  20.5 6.1 %collective-permute-start.2 = (f32[32,2304]{1,0:T(8,128)S(1)}, f32[32,2304]{1,0:T(8,128)S(1)}, u32[]{:S(2)}, u32[]{:S(2)}) collective-permute-start(f32[32,2304]{1,0:T(8,128)S(1)} %collective-permute-done.1), channel_id=1, source_target_pairs={{0,1},{1,2},{2,3},{3,0},{4,5},{5,6},{6,7},{7,4},{8,9},{9,10},{10,1... | collective-permute-start | bytes 884744 | tf_op jit(solution)/shard_map/ppermute | solution.py:16
  67.3 3.8 %copy-start = (f32[32,2304]{1,0:T(8,128)S(1)}, f32[32,2304]{1,0:T(8,128)}, u32[]{:S(2)}) copy-start(f32[32,2304]{1,0:T(8,128)} %param.6) | copy-start | bytes 884740
  67.3 32.2 %all-to-all-start = ((f32[32,4,4608]{2,0,1:T(8,128)}), f32[32,4,4608]{2,0,1:T(8,128)S(1)}, u32[]{:S(2)}, u32[]{:S(2)}) async-start(f32[32,4,4608]{2,0,1:T(8,128)} %bitcast.12), calls=%async_computation | async-start | bytes 4718592 | tf_op jit(solution)/shard_map/all_to_all | solution.py:22
Sparse Core Ops, SparseCore 0:
  9.5 54.5 all-gather.1
